TPU v7x, 256 devices: a whole 4x4x8 slice. The times are simulated.
256 devices in a mesh: dp: 4 (over x), expert: 64 (over z, y, core).
Axes of the slice: x: 4, y: 4, z: 8, core: 2. Of those that a mesh axis runs over, the one named last changes fastest.
Arguments:
- hidden_acts: bfloat16 [4, 64, 1024, 768], P('dp', 'expert'), may hold values from -6 to 6
- out_grads: bfloat16 [4, 64, 1024, 2048], P('dp', 'expert'), may hold values from -0.29882812 to 0.29882812
- row_counts: int32 [4, 64], P('dp', 'expert'), may hold values from 128 to 1024, as said below
- plan_now: int32 [4, 64], replicated, may hold values from 0 to 23, as said below
- plan_next: int32 [4, 64], replicated, may hold values from 0 to 23, as said below
- master: float32 [24, 768, 2048], P(None, 'expert', 'dp'), may hold values from -6 to 6
- moment_one: float32 [24, 768, 2048], P(None, 'expert', 'dp'), may hold values from -6 to 6
- moment_two: float32 [24, 768, 2048], P(None, 'expert', 'dp'), may hold values from 0.01 to 0.3
Outputs:
- master_new: float32 [24, 768, 2048], P(None, 'expert', 'dp')
- moment_one_new: float32 [24, 768, 2048], P(None, 'expert', 'dp')
- moment_two_new: float32 [24, 768, 2048], P(None, 'expert', 'dp')
- replica_weights: bfloat16 [4, 64, 768, 2048], P('dp', 'expert')
Inputs may be any that keep to these rules, and one draw needn't show every extreme that they name: `plan_now`: every expert is named by 1 to 16 devices, and some expert by exactly 16. `plan_next`: every expert is named by 1 to 16 devices, and some expert by exactly 16. `row_counts`: A multiple of 128; rows from it on are padding. Some device has all 1024 rows live.
All inputs are finite; a program needn't handle non-finite values.
Results may differ from a plain program's by a relative error of at most 0.005.
Values may be sent and summed in bfloat16 or wider, within the bound.
A program may use at most 64 MiB of HBM per device.

v0:
```python
import jax
import jax.numpy as jnp
from jax import lax
from jax.sharding import PartitionSpec as P

beta_one = 0.9
beta_two = 0.999
learn_rate = 0.1
epsilon = 1e-08
first_fix = 1.0 - beta_one**10
second_fix = 1.0 - beta_two**10


def per_device(
    hidden_acts, out_grads, row_counts, plan_now, plan_next, master, moment_one, moment_two
):
    ex_count = lax.axis_size("expert")
    dp_index = lax.axis_index("dp")
    experts = master.shape[0]
    piece_rows = master.shape[1]
    hidden = hidden_acts[0, 0]
    upstream = out_grads[0, 0]
    width = upstream.shape[1]
    row_index = jnp.arange(hidden.shape[0], dtype=jnp.int32)
    row_mask = (row_index < row_counts[0, 0]).astype(hidden.dtype)[:, None]
    partial_value = lax.dot_general(
        hidden * row_mask, upstream, (((0,), (0,)), ((), ())), preferred_element_type=jnp.float32
    ).astype(jnp.bfloat16)
    expert_ids = jnp.arange(experts, dtype=jnp.int32)
    pieces = lax.all_to_all(
        partial_value.reshape(ex_count, piece_rows, width),
        "expert",
        split_axis=0,
        concat_axis=0,
        tiled=True,
    )
    sender_ids = lax.dynamic_index_in_dim(plan_now, dp_index, 0, keepdims=False)
    onehot = (sender_ids[None, :] == expert_ids[:, None]).astype(jnp.bfloat16)
    totals = jnp.einsum("es,srd->erd", onehot, pieces, preferred_element_type=jnp.float32)
    grad_sum = lax.psum_scatter(
        totals.astype(jnp.bfloat16), "dp", scatter_dimension=2, tiled=True
    ).astype(jnp.float32)
    moment_one_new = beta_one * moment_one + (1.0 - beta_one) * grad_sum
    moment_two_new = beta_two * moment_two + (1.0 - beta_two) * grad_sum * grad_sum
    master_new = master - learn_rate * (moment_one_new / first_fix) / (
        jnp.sqrt(moment_two_new / second_fix) + epsilon
    )
    rounded = master_new.astype(jnp.bfloat16)
    full_cols = lax.all_gather(rounded, "dp", axis=2, tiled=True)
    targets = lax.dynamic_index_in_dim(plan_next, dp_index, 0, keepdims=False)
    outgoing = jnp.take(full_cols, targets, axis=0)
    incoming = lax.all_to_all(outgoing, "expert", split_axis=0, concat_axis=0, tiled=True)
    replica = incoming.reshape(ex_count * piece_rows, width)
    return (master_new, moment_one_new, moment_two_new, replica[None, None])


def solution(mesh):
    return jax.shard_map(
        per_device,
        mesh=mesh,
        in_specs=(
            P("dp", "expert", None, None),
            P("dp", "expert", None, None),
            P("dp", "expert"),
            P(),
            P(),
            P(None, "expert", "dp"),
            P(None, "expert", "dp"),
            P(None, "expert", "dp"),
        ),
        out_specs=(
            P(None, "expert", "dp"),
            P(None, "expert", "dp"),
            P(None, "expert", "dp"),
            P("dp", "expert", None, None),
        ),
        check_vma=False,
    )
```

profile of v0, /device:TPU:8, one launch (start us, length us, event | category | flops | bytes accessed | tf_op | source)
XLA Modules:
  0.0 311.3 jit_solution(10174371553919339833)
XLA Ops:
  7.2 0.0 copy-start
  7.9 6.2 %fusion.2 = bf16[768,2048]{1,0:T(8,128)(2,1)S(1)} fusion(bf16[1,1,1024,2048]{3,2,1,0:T(8,128)(2,1)} %param.9, bf16[1,1,1024,768]{3,2,1,0:T(8,128)(2,1)} %param.8, bf16[1024]{0:T(1024)(128)(2,1)S(1)} %fusion.18), kind=kOutput, calls=%fused_computation.4 | convolution fusion | flops 3223584768 | bytes 8914944 | tf_op jit(solution)/shard_map/dot_general | solution.py:26
  14.1 2.7 reshape.58
  16.8 12.3 %all-to-all-start = ((bf16[64,12,2048]{2,1,0:T(8,128)(2,1)}), bf16[64,12,2048]{2,1,0:T(8,128)(2,1)}, u32[]{:S(2)}, u32[]{:S(2)}) async-start(bf16[64,12,2048]{2,1,0:T(8,128)(2,1)} %reshape.58), calls=%async_computation | async-start | bytes 8388608 | tf_op jit(solution)/shard_map/all_to_all | solution.py:30
  29.1 0.0 copy-start.1
  29.1 0.0 copy-start.2
  29.1 0.0 copy-start.3
  29.1 0.0 reduce-scatter.2.cloned.1.call-start
  29.2 0.0 copy-done
  29.2 0.0 copy-start.4
  29.2 96.0 %all-to-all-done = bf16[64,12,2048]{2,1,0:T(8,128)(2,1)} async-done(((bf16[64,12,2048]{2,1,0:T(8,128)(2,1)}), bf16[64,12,2048]{2,1,0:T(8,128)(2,1)}, u32[]{:S(2)}, u32[]{:S(2)}) %all-to-all-start) | async-done | bytes 3145760 | tf_op jit(solution)/shard_map/all_to_all | solution.py:30
  125.2 6.6 %fusion.7 = bf16[24,12,2048]{2,0,1:T(8,128)(2,1)} fusion(bf16[64,12,2048]{2,1,0:T(8,128)(2,1)} %all-to-all-done, s32[64]{0:T(128)S(1)} %dynamic-slice_bitcast_fusion), kind=kOutput, calls=%fused_computation.7 | convolution fusion | flops 76088832 | bytes 4325632 | tf_op jit(solution)/shard_map/es,srd->erd/dot_general | solution.py:39
  131.9 0.0 reduce-scatter.2.cloned.1.call-update
  131.9 0.0 all-gather.2.cloned.1.call-start
  131.9 22.9 %reduce-scatter.2.cloned.1.call-done = bf16[24,12,512]{2,0,1:T(8,128)(2,1)} async-done(((bf16[24,12,2048]{2,0,1:T(8,128)(2,1)}), bf16[24,12,512]{2,0,1:T(8,128)(2,1)}) %reduce-scatter.2.cloned.1.call-update) | async-done | bytes 294928 | tf_op jit(solution)/shard_map/reduce_scatter | solution.py:40
  154.8 0.0 copy-done.1
  154.8 0.0 copy-done.2
  154.8 0.0 copy-done.3
  154.8 2.5 fusion.20
  157.4 0.0 all-gather.2.cloned.1.call-update
  157.4 0.0 copy-done.4
  157.5 26.8 %all-gather.2.cloned.1.call-done = bf16[24,12,2048]{2,0,1:T(8,128)(2,1)} async-done(((bf16[24,12,512]{2,0,1:T(8,128)(2,1)}), bf16[24,12,2048]{2,0,1:T(8,128)(2,1)}) %all-gather.2.cloned.1.call-update) | async-done | bytes 1179664 | tf_op jit(solution)/shard_map/all_gather | solution.py:49
  184.3 1.9 copy.16
  186.2 2.8 gather_fusion
  189.0 2.6 broadcast_select_fusion
  191.6 106.7 %all_to_all.10 = bf16[64,12,2048]{2,1,0:T(8,128)(2,1)} all-to-all(bf16[64,12,2048]{2,1,0:T(8,128)(2,1)S(1)} %broadcast_select_fusion), channel_id=1, replica_groups=mesh['dp'=4,'expert'=64] {'expert'}, dimensions={0} | all-to-all | bytes 6291456 | tf_op jit(solution)/shard_map/all_to_all | solution.py:52
  298.3 6.2 %broadcast_in_dim_reshape.3 = bf16[1,1,768,2048]{3,2,1,0:T(8,128)(2,1)} reshape(bf16[64,12,2048]{2,1,0:T(8,128)(2,1)} %all_to_all.10) | data formatting | bytes 6291456 | tf_op jit(solution)/shard_map/broadcast_in_dim;reshape | solution.py:54
  (5 shorter events, 0.0 us)
Async XLA Ops:
  7.2 22.0 %copy-start = (s32[4,64]{1,0:T(4,128)S(1)}, s32[4,64]{1,0:T(4,128)}, u32[]{:S(2)}) copy-start(s32[4,64]{1,0:T(4,128)} %param.11) | copy-start | bytes 3076
  16.8 108.4 %all-to-all-start = ((bf16[64,12,2048]{2,1,0:T(8,128)(2,1)}), bf16[64,12,2048]{2,1,0:T(8,128)(2,1)}, u32[]{:S(2)}, u32[]{:S(2)}) async-start(bf16[64,12,2048]{2,1,0:T(8,128)(2,1)} %reshape.58), calls=%async_computation | async-start | bytes 8388608 | tf_op jit(solution)/shard_map/all_to_all | solution.py:30
  29.1 125.7 %copy-start.1 = (f32[24,12,512]{2,0,1:T(8,128)S(1)}, f32[24,12,512]{2,0,1:T(8,128)}, u32[]{:S(2)}) copy-start(f32[24,12,512]{2,0,1:T(8,128)} %param.13) | copy-start | bytes 1769476
  29.1 125.7 %copy-start.2 = (f32[24,12,512]{2,0,1:T(8,128)S(1)}, f32[24,12,512]{2,0,1:T(8,128)}, u32[]{:S(2)}) copy-start(f32[24,12,512]{2,0,1:T(8,128)} %param.14) | copy-start | bytes 1769476
  29.1 125.7 %copy-start.3 = (f32[24,12,512]{2,0,1:T(8,128)S(1)}, f32[24,12,512]{2,0,1:T(8,128)}, u32[]{:S(2)}) copy-start(f32[24,12,512]{2,0,1:T(8,128)} %param.15) | copy-start | bytes 1769476
  29.1 125.7 %reduce-scatter.2.cloned.1.call-start = ((), (), s32[]{:S(2)}) async-start(), calls=%async_computation.3 | async-start | bytes 1474560 | tf_op jit(solution)/shard_map/reduce_scatter | solution.py:40
  29.2 128.2 %copy-start.4 = (s32[4,64]{1,0:T(4,128)S(1)}, s32[4,64]{1,0:T(4,128)}, u32[]{:S(2)}) copy-start(s32[4,64]{1,0:T(4,128)} %param.12) | copy-start | bytes 3076
  131.9 52.4 %all-gather.2.cloned.1.call-start = ((), (), s32[]{:S(2)}) async-start(), calls=%async_computation.4 | async-start | bytes 1474560 | tf_op jit(solution)/shard_map/all_gather | solution.py:49
Sparse Core Ops, SparseCore 0:
  132.0 22.7 reduce-scatter.1
  157.5 26.6 all-gather.1
where the time goes:
time: 312 us; the launch traced here: 311 us
  waiting for transfers between devices  146 us (47%)
  blocking collectives  107 us (34%)
  between operations  14.8 us (5%)
  local copies, waits for them, and re-layouts  13.6 us (4%)
  matrix products  12.9 us (4%)
  starting transfers between devices  12.4 us (4%)
  other arithmetic  5.2 us (2%)
    all_to_all x1, blocking collectives, per_device(): lax.all_to_all(outgoing, 'expert', split_axis=0, concat_axis=0, tiled=True)  107 us
    all_to_all x1, waiting for transfers between devices, per_device(): lax.all_to_all(partial_value.reshape(ex_count, piece_rows, width), 'exper...  96 us
    all_gather x1, waiting for transfers between devices, per_device(): full_cols = lax.all_gather(rounded, 'dp', axis=2, tiled=True)  26.8 us
    reduce_scatter x1, waiting for transfers between devices, per_device(): lax.psum_scatter(totals.astype(jnp.bfloat16), 'dp', scatter_dimension=2,...  22.9 us
    all_to_all x1, starting transfers between devices, per_device(): lax.all_to_all(partial_value.reshape(ex_count, piece_rows, width), 'exper...  12.3 us
    dot_general x1, matrix products, per_device(): jnp.einsum('es,srd->erd', onehot, pieces, preferred_element_type=jnp.floa...  6.64 us
  transfers between devices with their start and end apart: 3, of which 3 were waited for; matrix products, arithmetic and copies ran while one was open for 0% of the time, Pallas kernels for 0%

commit v1 on v0

--- a/solution.py
+++ b/solution.py
@@ -46,7 +46,24 @@
         jnp.sqrt(moment_two_new / second_fix) + epsilon
     )
     rounded = master_new.astype(jnp.bfloat16)
-    full_cols = lax.all_gather(rounded, "dp", axis=2, tiled=True)
+    peers, index, extent = (lax.axis_size("dp"), lax.axis_index("dp"), rounded.shape[2])
+    forward = [(i, (i + 1) % peers) for i in range(peers)]
+    left = [(i, (i - 1) % peers) for i in range(peers)]
+    out = jnp.zeros((*rounded.shape[:2], peers * extent, *rounded.shape[2 + 1 :]), rounded.dtype)
+    out = lax.dynamic_update_slice_in_dim(out, rounded, index * extent, axis=2)
+    from_left = from_right = rounded
+    half = peers // 2
+    for turn in range(1, half + 1):
+        from_left = lax.ppermute(from_left, "dp", forward)
+        out = lax.dynamic_update_slice_in_dim(
+            out, from_left, (index - turn) % peers * extent, axis=2
+        )
+        if turn < peers - half:
+            from_right = lax.ppermute(from_right, "dp", left)
+            out = lax.dynamic_update_slice_in_dim(
+                out, from_right, (index + turn) % peers * extent, axis=2
+            )
+    full_cols = out
     targets = lax.dynamic_index_in_dim(plan_next, dp_index, 0, keepdims=False)
     outgoing = jnp.take(full_cols, targets, axis=0)
     incoming = lax.all_to_all(outgoing, "expert", split_axis=0, concat_axis=0, tiled=True)

time: 312 us -> 300 us (0.962)
  waiting for transfers between devices: 146 us -> 132 us
  starting transfers between devices: 12.4 us -> 15.6 us
    all_gather x1 -> x0, waiting for transfers between devices: 26.8 us -> none  [per_device(): full_cols = lax.all_gather(rounded, 'dp', axis=2, tiled=True)]
    ppermute x0 -> x3, waiting for transfers between devices: none -> 12.8 us  [the longest x2 12.8 us: per_device(): from_left = lax.ppermute(from_left, 'dp', forward)]
    ppermute x0 -> x3, starting transfers between devices: none -> 3.32 us  [the longest x1 3.31 us: per_device(): from_right = lax.ppermute(from_right, 'dp', left)]
  transfers between devices with their start and end apart: 3 -> 5, of which waited for: 3 -> 4; matrix products, arithmetic and copies ran while one was open for 0% -> 0% of each run, Pallas kernels for 0% -> 0%
where the time goes in v1:
time: 300 us; the launch traced here: 299 us
  waiting for transfers between devices  132 us (44%)
  blocking collectives  107 us (36%)
  starting transfers between devices  15.6 us (5%)
  between operations  14.9 us (5%)
  matrix products  12.9 us (4%)
  local copies, waits for them, and re-layouts  12.3 us (4%)
  other arithmetic  5.1 us (2%)
    all_to_all x1, blocking collectives, per_device(): lax.all_to_all(outgoing, 'expert', split_axis=0, concat_axis=0, tiled=True)  107 us
    all_to_all x1, waiting for transfers between devices, per_device(): lax.all_to_all(partial_value.reshape(ex_count, piece_rows, width), 'exper...  96 us
    reduce_scatter x1, waiting for transfers between devices, per_device(): lax.psum_scatter(totals.astype(jnp.bfloat16), 'dp', scatter_dimension=2,...  22.9 us
    ppermute x2, waiting for transfers between devices, per_device(): from_left = lax.ppermute(from_left, 'dp', forward)  12.8 us
    all_to_all x1, starting transfers between devices, per_device(): lax.all_to_all(partial_value.reshape(ex_count, piece_rows, width), 'exper...  12.3 us
    dot_general x1, matrix products, per_device(): jnp.einsum('es,srd->erd', onehot, pieces, preferred_element_type=jnp.floa...  6.64 us
    dot_general x1, matrix products, per_device(): lax.dot_general(hidden * row_mask, upstream, (((0,), (0,)), ((), ())), pr...  6.23 us
    another operation x1, local copies, waits for them, and re-layouts, per_device(): return (master_new, moment_one_new, moment_two_new, replica[None, None])  6.15 us
  transfers between devices with their start and end apart: 5, of which 4 were waited for; matrix products, arithmetic and copies ran while one was open for 0% of the time, Pallas kernels for 0%

profile of v1, /device:TPU:8, one launch (start us, length us, event | category | flops | bytes accessed | tf_op | source)
XLA Modules:
  0.0 299.2 jit_solution(3391603351303924301)
XLA Ops:
  7.2 0.0 copy-start
  7.9 6.2 %fusion.2 = bf16[768,2048]{1,0:T(8,128)(2,1)S(1)} fusion(bf16[1,1,1024,2048]{3,2,1,0:T(8,128)(2,1)} %param.9, bf16[1,1,1024,768]{3,2,1,0:T(8,128)(2,1)} %param.8, bf16[1024]{0:T(1024)(128)(2,1)S(1)} %fusion.18), kind=kOutput, calls=%fused_computation.4 | convolution fusion | flops 3223584768 | bytes 8914944 | tf_op jit(solution)/shard_map/dot_general | solution.py:26
  14.1 2.7 reshape.58
  16.8 12.3 %all-to-all-start = ((bf16[64,12,2048]{2,1,0:T(8,128)(2,1)}), bf16[64,12,2048]{2,1,0:T(8,128)(2,1)}, u32[]{:S(2)}, u32[]{:S(2)}) async-start(bf16[64,12,2048]{2,1,0:T(8,128)(2,1)} %reshape.58), calls=%async_computation | async-start | bytes 8388608 | tf_op jit(solution)/shard_map/all_to_all | solution.py:30
  29.1 0.0 reduce-scatter.2.cloned.1.call-start
  29.2 0.0 copy-done
  29.2 0.0 copy-start.4
  29.2 0.0 copy-start.1
  29.2 0.0 copy-start.2
  29.2 0.0 copy-start.3
  29.2 96.0 %all-to-all-done = bf16[64,12,2048]{2,1,0:T(8,128)(2,1)} async-done(((bf16[64,12,2048]{2,1,0:T(8,128)(2,1)}), bf16[64,12,2048]{2,1,0:T(8,128)(2,1)}, u32[]{:S(2)}, u32[]{:S(2)}) %all-to-all-start) | async-done | bytes 3145760 | tf_op jit(solution)/shard_map/all_to_all | solution.py:30
  125.2 6.6 %fusion.7 = bf16[24,12,2048]{2,0,1:T(8,128)(2,1)} fusion(bf16[64,12,2048]{2,1,0:T(8,128)(2,1)} %all-to-all-done, s32[64]{0:T(128)S(1)} %fusion.19), kind=kOutput, calls=%fused_computation.7 | convolution fusion | flops 76088832 | bytes 4325632 | tf_op jit(solution)/shard_map/es,srd->erd/dot_general | solution.py:39
  131.9 0.0 reduce-scatter.2.cloned.1.call-update
  131.9 0.0 copy-done.4
  131.9 22.9 %reduce-scatter.2.cloned.1.call-done = bf16[24,12,512]{2,0,1:T(8,128)(2,1)} async-done(((bf16[24,12,2048]{2,0,1:T(8,128)(2,1)}), bf16[24,12,512]{2,0,1:T(8,128)(2,1)}) %reduce-scatter.2.cloned.1.call-update) | async-done | bytes 294928 | tf_op jit(solution)/shard_map/reduce_scatter | solution.py:40
  154.8 0.0 copy-done.1
  154.8 2.4 fusion.21
  157.3 0.0 collective-permute-start
  157.4 3.3 %collective-permute-start.1 = (bf16[24,12,512]{2,0,1:T(8,128)(2,1)S(1)}, bf16[24,12,512]{2,0,1:T(8,128)(2,1)S(1)}, u32[]{:S(2)}, u32[]{:S(2)}) collective-permute-start(bf16[24,12,512]{2,0,1:T(8,128)(2,1)S(1)} %get-tuple-element.4), channel_id=1, source_target_pairs={{0,192},{64,0},{128,64},{192,128},{1,193},{65,1},{129,65},{193,129... | collective-permute-start | bytes 884744 | tf_op jit(solution)/shard_map/ppermute | solution.py:62
  160.7 0.2 broadcast_in_dim.17
  160.9 0.1 copy_dynamic-update-slice_fusion.3
  161.0 5.1 %collective-permute-done = bf16[24,12,512]{2,0,1:T(8,128)(2,1)S(1)} collective-permute-done((bf16[24,12,512]{2,0,1:T(8,128)(2,1)S(1)}, bf16[24,12,512]{2,0,1:T(8,128)(2,1)S(1)}, u32[]{:S(2)}, u32[]{:S(2)}) %collective-permute-start) | collective-permute-done | bytes 294944 | tf_op jit(solution)/shard_map/ppermute | solution.py:57
  166.1 0.0 collective-permute-start.2
  166.1 0.1 copy_dynamic-update-slice_fusion.2
  166.2 0.0 collective-permute-done.1
  166.2 0.1 copy_dynamic-update-slice_fusion.1
  166.3 7.7 %collective-permute-done.2 = bf16[24,12,512]{2,0,1:T(8,128)(2,1)S(1)} collective-permute-done((bf16[24,12,512]{2,0,1:T(8,128)(2,1)S(1)}, bf16[24,12,512]{2,0,1:T(8,128)(2,1)S(1)}, u32[]{:S(2)}, u32[]{:S(2)}) %collective-permute-start.2) | collective-permute-done | bytes 294944 | tf_op jit(solution)/shard_map/ppermute | solution.py:57
  174.0 0.1 copy_dynamic-update-slice_fusion
  174.1 2.8 gather_fusion
  176.9 2.6 broadcast_select_fusion
  179.5 106.7 %all_to_all.10 = bf16[64,12,2048]{2,1,0:T(8,128)(2,1)} all-to-all(bf16[64,12,2048]{2,1,0:T(8,128)(2,1)S(1)} %broadcast_select_fusion), channel_id=1, replica_groups=mesh['dp'=4,'expert'=64] {'expert'}, dimensions={0} | all-to-all | bytes 6291456 | tf_op jit(solution)/shard_map/all_to_all | solution.py:69
  286.2 6.2 %broadcast_in_dim_reshape.3 = bf16[1,1,768,2048]{3,2,1,0:T(8,128)(2,1)} reshape(bf16[64,12,2048]{2,1,0:T(8,128)(2,1)} %all_to_all.10) | data formatting | bytes 6291456 | tf_op jit(solution)/shard_map/broadcast_in_dim;reshape | solution.py:71
  (7 shorter events, 0.0 us)
Async XLA Ops:
  7.2 22.0 %copy-start = (s32[4,64]{1,0:T(4,128)S(1)}, s32[4,64]{1,0:T(4,128)}, u32[]{:S(2)}) copy-start(s32[4,64]{1,0:T(4,128)} %param.11) | copy-start | bytes 3076
  16.8 108.4 %all-to-all-start = ((bf16[64,12,2048]{2,1,0:T(8,128)(2,1)}), bf16[64,12,2048]{2,1,0:T(8,128)(2,1)}, u32[]{:S(2)}, u32[]{:S(2)}) async-start(bf16[64,12,2048]{2,1,0:T(8,128)(2,1)} %reshape.58), calls=%async_computation | async-start | bytes 8388608 | tf_op jit(solution)/shard_map/all_to_all | solution.py:30
  29.1 125.7 %reduce-scatter.2.cloned.1.call-start = ((), (), s32[]{:S(2)}) async-start(), calls=%async_computation.3 | async-start | bytes 1474560 | tf_op jit(solution)/shard_map/reduce_scatter | solution.py:40
  29.2 102.7 %copy-start.4 = (s32[4,64]{1,0:T(4,128)S(1)}, s32[4,64]{1,0:T(4,128)}, u32[]{:S(2)}) copy-start(s32[4,64]{1,0:T(4,128)} %param.12) | copy-start | bytes 3076
  29.2 125.6 %copy-start.1 = (f32[24,12,512]{2,0,1:T(8,128)S(1)}, f32[24,12,512]{2,0,1:T(8,128)}, u32[]{:S(2)}) copy-start(f32[24,12,512]{2,0,1:T(8,128)} %param.13) | copy-start | bytes 1769476
  29.2 125.6 %copy-start.2 = (f32[24,12,512]{2,0,1:T(8,128)S(1)}, f32[24,12,512]{2,0,1:T(8,128)}, u32[]{:S(2)}) copy-start(f32[24,12,512]{2,0,1:T(8,128)} %param.14) | copy-start | bytes 1769476
  29.2 125.6 %copy-start.3 = (f32[24,12,512]{2,0,1:T(8,128)S(1)}, f32[24,12,512]{2,0,1:T(8,128)}, u32[]{:S(2)}) copy-start(f32[24,12,512]{2,0,1:T(8,128)} %param.15) | copy-start | bytes 1769476
  157.3 8.8 %collective-permute-start = (bf16[24,12,512]{2,0,1:T(8,128)(2,1)S(1)}, bf16[24,12,512]{2,0,1:T(8,128)(2,1)S(1)}, u32[]{:S(2)}, u32[]{:S(2)}) collective-permute-start(bf16[24,12,512]{2,0,1:T(8,128)(2,1)S(1)} %get-tuple-element.4), channel_id=1, source_target_pairs={{0,64},{64,128},{128,192},{192,0},{1,65},{65,129},{129,193},{193,1... | collective-permute-start | bytes 884744 | tf_op jit(solution)/shard_map/ppermute | solution.py:57
  157.4 8.8 %collective-permute-start.1 = (bf16[24,12,512]{2,0,1:T(8,128)(2,1)S(1)}, bf16[24,12,512]{2,0,1:T(8,128)(2,1)S(1)}, u32[]{:S(2)}, u32[]{:S(2)}) collective-permute-start(bf16[24,12,512]{2,0,1:T(8,128)(2,1)S(1)} %get-tuple-element.4), channel_id=1, source_target_pairs={{0,192},{64,0},{128,64},{192,128},{1,193},{65,1},{129,65},{193,129... | collective-permute-start | bytes 884744 | tf_op jit(solution)/shard_map/ppermute | solution.py:62
  166.1 7.9 %collective-permute-start.2 = (bf16[24,12,512]{2,0,1:T(8,128)(2,1)S(1)}, bf16[24,12,512]{2,0,1:T(8,128)(2,1)S(1)}, u32[]{:S(2)}, u32[]{:S(2)}) collective-permute-start(bf16[24,12,512]{2,0,1:T(8,128)(2,1)S(1)} %collective-permute-done), channel_id=1, source_target_pairs={{0,64},{64,128},{128,192},{192,0},{1,65},{65,129},{129,193},{193,1... | collective-permute-start | bytes 884744 | tf_op jit(solution)/shard_map/ppermute | solution.py:57
Sparse Core Ops, SparseCore 0:
  132.0 22.7 reduce-scatter.1
